TPU v7x, 512 devices: a whole 4x4x16 slice. The times are simulated.
512 devices in a mesh: row: 64 (over x, z), col: 8 (over y, core).
Axes of the slice: x: 4, y: 4, z: 16, core: 2. Of those that a mesh axis runs over, the one named last changes fastest.
Arguments:
- pending: bfloat16 [65536, 8, 1024], P('row', 'col'), may hold values from -5 to 5
- panel: bfloat16 [65536, 2, 1024], P('row', None, 'col'), may hold values from -0.1875 to 0.1875
- panel_scale: float32 [65536, 2], P('row'), may hold values from 0.1 to 1
- inverse_blocks: bfloat16 [2, 1024, 1024], P(None, 'col'), as said below
Outputs:
- remaining: bfloat16 [65536, 8, 1024], P('row', 'col')
- solved: bfloat16 [2, 1024, 1024], P(None, 'col')
Inputs may be any that keep to these rules, and one draw needn't show every extreme that they name: `inverse_blocks`: each block is lower triangular with a positive diagonal, the inverse of a diagonal block of a Cholesky factor.
All inputs are finite; a program needn't handle non-finite values.
Results may differ from a plain program's by a relative error of at most 0.023.
Values may be sent and summed in bfloat16 or wider, within the bound.
A program may use at most 64 MiB of HBM per device.

v0:
```python
import jax
import jax.numpy as jnp
from jax import lax
from jax.sharding import PartitionSpec as P


def spread(shard, axis, root):
    mine = lax.axis_index(axis) == root
    return lax.psum(jnp.where(mine, shard, jnp.zeros_like(shard)), axis)


def body(pending, panel, panel_scale, inverse_blocks):
    row_index = lax.axis_index("row")
    n_row = lax.axis_size("row")
    block = inverse_blocks.shape[2]
    total = pending.shape[0]
    current = pending[:, 0, :]
    slot_of_row = lax.broadcasted_iota(jnp.int32, (total,), 0) // block
    global_ids = slot_of_row * n_row + row_index
    solved_list = []
    for k in range(2):
        head = current.astype(jnp.float32)
        fan = lax.psum(head.astype(jnp.bfloat16), "col")
        local = jnp.dot(inverse_blocks[k], fan, preferred_element_type=jnp.float32).astype(
            jnp.bfloat16
        )
        arrived = spread(local, "row", k)
        solved_list.append(arrived)
        term = jnp.dot(panel[:, k, :], arrived, preferred_element_type=jnp.float32)
        newer = (current.astype(jnp.float32) - panel_scale[:, k : k + 1] * term).astype(
            jnp.bfloat16
        )
        current = jnp.where((global_ids > k)[:, None], newer, current)
    return (current[:, None, :], jnp.stack(solved_list))


def solution(mesh):
    placed = (P("row", "col", None), P("row", None, "col"), P("row", None), P(None, "col", None))
    return jax.shard_map(
        body,
        mesh=mesh,
        in_specs=placed,
        out_specs=(P("row", "col", None), P(None, "col", None)),
        check_vma=False,
    )
```

profile of v0, /device:TPU:8, one launch (start us, length us, event | category | flops | bytes accessed | tf_op | source)
XLA Modules:
  0.0 722.6 jit_solution(12241897476524964744)
XLA Ops:
  7.2 0.0 all-reduce.5.cloned.1.call-start
  7.2 3.9 copy.9
  11.2 0.0 copy-start.7
  11.2 0.0 copy-start.5
  11.2 0.0 copy-start.2
  11.2 0.0 all-reduce.5.cloned.1.call-update
  11.2 0.0 all-reduce.7.cloned.1.call-start
  11.3 0.6 copy-done.7
  11.9 0.0 copy-start
  11.9 82.6 %all-reduce.5.cloned.1.call-done = bf16[1024,1024]{0,1:T(8,128)(2,1)} async-done(((bf16[1024,1024]{0,1:T(8,128)(2,1)}), bf16[1024,1024]{0,1:T(8,128)(2,1)}) %all-reduce.5.cloned.1.call-update) | async-done | bytes 2097168 | tf_op jit(solution)/shard_map/psum | solution.py:23
  94.5 0.0 copy-done.5
  94.5 3.1 fusion.5
  97.6 0.0 all-reduce.7.cloned.1.call-update
  97.6 0.0 all-reduce.9.cloned.1.call-start
  97.7 0.0 copy-done.2
  97.7 1.5 fusion.19
  99.2 263.4 %all-reduce.7.cloned.1.call-done = bf16[128,1024]{1,0:T(8,128)(2,1)} async-done(((bf16[128,1024]{1,0:T(8,128)(2,1)}), bf16[128,1024]{1,0:T(8,128)(2,1)}) %all-reduce.7.cloned.1.call-update) | async-done | bytes 262160 | tf_op jit(solution)/shard_map/psum | solution.py:9
  362.6 0.0 copy-done
  362.6 3.3 fusion.2
  365.9 0.0 copy-start.6
  365.9 0.0 all-reduce.9.cloned.1.call-update
  365.9 0.0 copy-start.1
  365.9 0.0 all-reduce.11.cloned.1.call-start
  366.0 73.2 %all-reduce.9.cloned.1.call-done = bf16[1024,1024]{0,1:T(8,128)(2,1)} async-done(((bf16[1024,1024]{0,1:T(8,128)(2,1)}), bf16[1024,1024]{0,1:T(8,128)(2,1)}) %all-reduce.9.cloned.1.call-update) | async-done | bytes 2097168 | tf_op jit(solution)/shard_map/psum | solution.py:23
  439.2 0.0 copy-done.6
  439.2 3.1 fusion.7
  442.3 0.0 all-reduce.11.cloned.1.call-update
  442.4 265.7 %all-reduce.11.cloned.1.call-done = bf16[128,1024]{1,0:T(8,128)(2,1)} async-done(((bf16[128,1024]{1,0:T(8,128)(2,1)}), bf16[128,1024]{1,0:T(8,128)(2,1)}) %all-reduce.11.cloned.1.call-update) | async-done | bytes 262160 | tf_op jit(solution)/shard_map/psum | solution.py:9
  708.1 0.0 copy-done.1
  708.1 3.1 fusion.4
  711.3 0.0 copy-start.3
  711.3 0.0 copy-start.4
  711.3 4.0 copy.13
  715.3 0.0 copy-done.3
  715.3 0.0 copy-done.4
  715.3 0.8 pad_maximum_fusion
  (3 shorter events, 0.0 us)
Async XLA Ops:
  7.2 87.3 %all-reduce.5.cloned.1.call-start = ((), (), s32[]{:S(2)}) async-start(), calls=%async_computation | async-start | bytes 4194304 | tf_op jit(solution)/shard_map/psum | solution.py:23
  11.2 0.7 copy-start.7
  11.2 83.3 %copy-start.5 = (bf16[2,128,1024]{2,1,0:T(8,128)(2,1)S(1)}, bf16[2,128,1024]{2,1,0:T(8,128)(2,1)}, u32[]{:S(2)}) copy-start(bf16[2,128,1024]{2,1,0:T(8,128)(2,1)} %param.7) | copy-start | bytes 1572868
  11.2 86.5 %copy-start.2 = (bf16[1024,2,128]{2,1,0:T(2,128)(2,1)S(1)}, bf16[1024,2,128]{2,1,0:T(2,128)(2,1)}, u32[]{:S(2)}) copy-start(bf16[1024,2,128]{2,1,0:T(2,128)(2,1)} %param.5) | copy-start | bytes 1572868
  11.2 351.4 %all-reduce.7.cloned.1.call-start = ((), (), s32[]{:S(2)}) async-start(), calls=%async_computation.1 | async-start | bytes 524288 | tf_op jit(solution)/shard_map/psum | solution.py:9
  11.9 350.7 %copy-start = (bf16[1024,1,1024]{0,2,1:T(8,128)(2,1)S(1)}, bf16[1024,1,1024]{0,2,1:T(8,128)(2,1)}, u32[]{:S(2)}) copy-start(bf16[1024,1,1024]{0,2,1:T(8,128)(2,1)} %copy.9) | copy-start | bytes 6291460
  97.6 341.6 %all-reduce.9.cloned.1.call-start = ((), (), s32[]{:S(2)}) async-start(), calls=%async_computation.2 | async-start | bytes 4194304 | tf_op jit(solution)/shard_map/psum | solution.py:23
  365.9 73.3 %copy-start.6 = (bf16[2,128,1024]{2,1,0:T(8,128)(2,1)S(1)}, bf16[2,128,1024]{2,1,0:T(8,128)(2,1)}, u32[]{:S(2)}) copy-start(bf16[2,128,1024]{2,1,0:T(8,128)(2,1)} %param.7) | copy-start | bytes 1572868
  365.9 342.2 %copy-start.1 = (bf16[1024,1024]{0,1:T(8,128)(2,1)S(1)}, bf16[1024,1024]{0,1:T(8,128)(2,1)}, u32[]{:S(2)}) copy-start(bf16[1024,1024]{0,1:T(8,128)(2,1)} %fusion.2) | copy-start | bytes 6291460
  365.9 342.2 %all-reduce.11.cloned.1.call-start = ((), (), s32[]{:S(2)}) async-start(), calls=%async_computation.3 | async-start | bytes 524288 | tf_op jit(solution)/shard_map/psum | solution.py:9
  711.3 4.0 copy-start.3
  711.3 4.0 copy-start.4
Sparse Core Ops, SparseCore 0:
  11.3 83.1 all-reduce.4
  97.9 264.6 all-reduce.6
  366.0 73.1 all-reduce.8
  443.5 264.6 all-reduce.10
where the time goes:
time: 723 us
  waiting for transfers between devices  685 us (95%)
  between operations  13.8 us (2%)
  matrix products  12.7 us (2%)
  local copies, waits for them, and re-layouts  10.1 us (1%)
    psum x2, waiting for transfers between devices, spread(): return lax.psum(jnp.where(mine, shard, jnp.zeros_like(shard)), axis)  529 us
    psum x2, waiting for transfers between devices, body(): fan = lax.psum(head.astype(jnp.bfloat16), 'col')  156 us
  transfers between devices with their start and end apart: 4, of which 4 were waited for; matrix products, arithmetic and copies ran while one was open for 0% of the time, Pallas kernels for 0%

commit v1 on v0

--- a/solution.py
+++ b/solution.py
@@ -6,7 +6,7 @@
 
 def spread(shard, axis, root):
     mine = lax.axis_index(axis) == root
-    return lax.psum(jnp.where(mine, shard, jnp.zeros_like(shard)), axis)
+    return jnp.sum(lax.all_gather(jnp.where(mine, shard, jnp.zeros_like(shard)), axis), axis=0)
 
 
 def body(pending, panel, panel_scale, inverse_blocks):

time: 723 us -> 636 us (0.88)
  the two profiles are of different devices: /device:TPU:8 before, /device:TPU:2 now
where the time goes in v1:
time: 636 us; the launch traced here: 635 us
  waiting for transfers between devices  574 us (90%)
  other arithmetic  18.5 us (3%)
  local copies, waits for them, and re-layouts  18.4 us (3%)
  between operations  13.9 us (2%)
  matrix products  10.5 us (2%)
    all_gather x2, waiting for transfers between devices, spread(): lax.all_gather(jnp.where(mine, shard, jnp.zeros_like(shard)), axis)  409 us
    psum x2, waiting for transfers between devices, body(): fan = lax.psum(head.astype(jnp.bfloat16), 'col')  165 us
    reduce_sum x2, other arithmetic, spread(): jnp.sum(lax.all_gather(jnp.where(mine, shard, jnp.zeros_like(shard)), axi...  17.6 us
    unnamed x15, local copies, waits for them, and re-layouts  17.6 us
  transfers between devices with their start and end apart: 4, of which 4 were waited for; matrix products, arithmetic and copies ran while one was open for 0% of the time, Pallas kernels for 0%

profile of v1, /device:TPU:2, one launch (start us, length us, event | category | flops | bytes accessed | tf_op | source)
XLA Modules:
  0.0 635.3 jit_solution(14211045408822969333)
XLA Ops:
  7.2 0.0 all-reduce.3.cloned.1.call-start
  7.2 3.9 copy.17
  11.2 0.0 copy-start.3
  11.2 0.0 copy-start.5
  11.2 0.0 copy-start.2
  11.2 0.0 all-reduce.3.cloned.1.call-update
  11.2 0.0 all-gather.5.cloned.1.call-start
  11.2 85.7 %all-reduce.3.cloned.1.call-done = bf16[1024,1024]{0,1:T(8,128)(2,1)} async-done(((bf16[1024,1024]{0,1:T(8,128)(2,1)}), bf16[1024,1024]{0,1:T(8,128)(2,1)}) %all-reduce.3.cloned.1.call-update) | async-done | bytes 2097168 | tf_op jit(solution)/shard_map/psum | solution.py:23
  96.9 0.0 copy-done.3
  96.9 3.1 fusion.5
  100.1 0.0 all-gather.5.cloned.1.call-update
  100.1 0.0 all-reduce.5.cloned.1.call-start
  100.2 0.0 copy-done.5
  100.2 0.0 copy-done.2
  100.2 0.7 fusion.19
  100.9 191.6 %all-gather.5.cloned.1.call-done = bf16[8192,1024]{1,0:T(8,128)(2,1)} async-done(((bf16[128,1024]{1,0:T(8,128)(2,1)}), bf16[8192,1024]{1,0:T(8,128)(2,1)}) %all-gather.5.cloned.1.call-update) | async-done | bytes 16777232 | tf_op jit(solution)/shard_map/all_gather | solution.py:9
  292.5 0.0 copy-start
  292.5 9.1 %reduce_sum.24 = bf16[128,1024]{1,0:T(8,128)(2,1)S(1)} reduce(bf16[64,128,1024]{2,1,0:T(8,128)(2,1)} %bitcast.46, bf16[]{:T(256)} %constant.36.clone.1), dimensions={0}, to_apply=%region_1.2 | reduce | flops 8257536 | bytes 17039362 | tf_op jit(solution)/shard_map/reduce_sum | solution.py:9
  301.6 0.0 copy-done
  301.6 2.2 fusion.2
  303.8 0.0 copy-start.4
  303.8 0.0 all-reduce.5.cloned.1.call-update
  303.8 0.0 all-gather.7.cloned.1.call-start
  303.9 78.9 %all-reduce.5.cloned.1.call-done = bf16[1024,1024]{0,1:T(8,128)(2,1)} async-done(((bf16[1024,1024]{0,1:T(8,128)(2,1)}), bf16[1024,1024]{0,1:T(8,128)(2,1)}) %all-reduce.5.cloned.1.call-update) | async-done | bytes 2097168 | tf_op jit(solution)/shard_map/psum | solution.py:23
  382.8 0.0 copy-done.4
  382.8 3.0 fusion.7
  385.8 0.0 all-gather.7.cloned.1.call-update
  385.8 217.6 %all-gather.7.cloned.1.call-done = bf16[8192,1024]{0,1:T(8,128)(2,1)} async-done(((bf16[128,1024]{0,1:T(8,128)(2,1)}), bf16[8192,1024]{0,1:T(8,128)(2,1)}) %all-gather.7.cloned.1.call-update) | async-done | bytes 16777232 | tf_op jit(solution)/shard_map/all_gather | solution.py:9
  603.4 9.7 %copy.24 = bf16[128,8,64,128]{3,2,1,0:T(8,128)(2,1)S(1)} copy(bf16[128,8,64,128]{3,1,2,0:T(8,128)(2,1)} %bitcast.47) | data formatting | bytes 33554432
  613.1 0.0 copy-start.1
  613.1 8.5 %bitcast_reduce_fusion = bf16[128,1024]{0,1:T(8,128)(2,1)S(1)} fusion(bf16[128,8,64,128]{3,2,1,0:T(8,128)(2,1)S(1)} %copy.24), kind=kLoop, calls=%fused_computation | loop fusion | flops 8257536 | bytes 17039360 | tf_op jit(solution)/shard_map/reduce_sum | solution.py:9
  621.6 0.1 copy.20
  621.8 0.0 copy-done.1
  621.8 2.2 fusion.4
  623.9 3.9 copy.21
  627.9 0.8 pad_maximum_fusion
  (3 shorter events, 0.0 us)
Async XLA Ops:
  7.2 89.8 %all-reduce.3.cloned.1.call-start = ((), (), s32[]{:S(2)}) async-start(), calls=%async_computation | async-start | bytes 4194304 | tf_op jit(solution)/shard_map/psum | solution.py:23
  11.2 85.8 %copy-start.3 = (bf16[2,128,1024]{2,1,0:T(8,128)(2,1)S(1)}, bf16[2,128,1024]{2,1,0:T(8,128)(2,1)}, u32[]{:S(2)}) copy-start(bf16[2,128,1024]{2,1,0:T(8,128)(2,1)} %param.7) | copy-start | bytes 1572868
  11.2 89.0 %copy-start.5 = (f32[1024,2]{0,1:T(2,128)S(1)}, f32[1024,2]{0,1:T(2,128)}, u32[]{:S(2)}) copy-start(f32[1024,2]{0,1:T(2,128)} %param.6) | copy-start | bytes 24580
  11.2 89.0 %copy-start.2 = (bf16[1024,2,128]{2,1,0:T(2,128)(2,1)S(1)}, bf16[1024,2,128]{2,1,0:T(2,128)(2,1)}, u32[]{:S(2)}) copy-start(bf16[1024,2,128]{2,1,0:T(2,128)(2,1)} %param.5) | copy-start | bytes 1572868
  11.2 281.3 %all-gather.5.cloned.1.call-start = ((), (), s32[]{:S(2)}) async-start(), calls=%async_computation.2 | async-start | bytes 17039360 | tf_op jit(solution)/shard_map/all_gather | solution.py:9
  100.1 282.7 %all-reduce.5.cloned.1.call-start = ((), (), s32[]{:S(2)}) async-start(), calls=%async_computation.1 | async-start | bytes 4194304 | tf_op jit(solution)/shard_map/psum | solution.py:23
  292.5 9.1 %copy-start = (bf16[1024,1,1024]{0,2,1:T(8,128)(2,1)S(1)}, bf16[1024,1,1024]{0,2,1:T(8,128)(2,1)}, u32[]{:S(2)}) copy-start(bf16[1024,1,1024]{0,2,1:T(8,128)(2,1)} %copy.17) | copy-start | bytes 6291460
  303.8 79.0 %copy-start.4 = (bf16[2,128,1024]{2,1,0:T(8,128)(2,1)S(1)}, bf16[2,128,1024]{2,1,0:T(8,128)(2,1)}, u32[]{:S(2)}) copy-start(bf16[2,128,1024]{2,1,0:T(8,128)(2,1)} %param.7) | copy-start | bytes 1572868
  303.8 299.6 %all-gather.7.cloned.1.call-start = ((), (), s32[]{:S(2)}) async-start(), calls=%async_computation.3 | async-start | bytes 17039360 | tf_op jit(solution)/shard_map/all_gather | solution.py:9
  613.1 8.7 %copy-start.1 = (bf16[1024,1024]{0,1:T(8,128)(2,1)S(1)}, bf16[1024,1024]{0,1:T(8,128)(2,1)}, u32[]{:S(2)}) copy-start(bf16[1024,1024]{0,1:T(8,128)(2,1)} %fusion.2) | copy-start | bytes 6291460
Sparse Core Ops, SparseCore 0:
  11.3 85.5 all-reduce.2
  100.5 191.9 all-gather.4
  304.0 78.7 all-reduce.4
  386.1 217.2 all-gather.6
